TPU v7x, 256 devices: a whole 4x4x8 slice. The times are simulated.
256 devices in a mesh: elem: 64 (over y, z, core), snap: 4 (over x).
Axes of the slice: x: 4, y: 4, z: 8, core: 2. Of those that a mesh axis runs over, the one named last changes fastest.
Arguments:
- node_basis: bfloat16 [65536, 1536], P('elem'), may hold values from -0.25 to 0.25
- stiff_terms: bfloat16 [16, 24, 24], replicated, may hold values from -1.25 to 1.25
- reduced_coords: bfloat16 [512, 32], P(None, 'snap'), may hold values from -6 to 6
- sample_list: int32 [512], replicated, may hold values from 0 to 2047, as said below
- connectivity: int32 [2048, 8], replicated, may hold values from -1 to 65535, as said below
- node_slot: int32 [65536], replicated, may hold values from 0 to 65535, as said below
- elem_device: int32 [512], replicated, may hold values from 0 to 63, as said below
Outputs:
- ortho_panel: float32 [1024, 512, 512], P('elem', 'snap')
- triangle_factor: float32 [512, 512], P('elem')
Inputs may be any that keep to these rules, and one draw needn't show every extreme that they name: `sample_list`: distinct element ids. `connectivity`: each element lists 4, 6 or 8 live nodes first and -1 after them; the live nodes of one element are owned by distinct indices of elem (owner = node_slot // 1024); for every index d of elem and every owner o, at most 2 sampled elements computed on d have a live node owned by o, and some pair (d, o) reaches 2. `node_slot`: a permutation. `elem_device`: each index of elem computes at most 16 sampled elements; some index computes exactly 16.
All inputs are finite; a program needn't handle non-finite values.
Results may differ from a plain program's by a relative error of at most 0.0056.
Values may be sent and summed in bfloat16 or wider, within the bound.
A program may use at most 64 MiB of HBM per device.

v0:
```python
import jax
import jax.numpy as jnp
from jax import lax
from jax.sharding import PartitionSpec as P

MODES = 512
ENODES = 8
NDOF = 3


def shards(
    node_basis, stiff_terms, reduced_coords, sample_list, connectivity, node_slot, elem_device
):
    devices = lax.axis_size("elem")
    elem_rank = lax.axis_index("elem")
    node_rows = node_basis.shape[0]
    sampled = sample_list.shape[0]
    capacity = 2 * sampled // devices
    pair_bound = (capacity * ENODES + devices - 1) // devices
    node_ids = connectivity[sample_list]
    live_nodes = node_ids >= 0
    stored_rows = jnp.where(live_nodes, node_slot[jnp.maximum(node_ids, 0)], 0)
    owners = stored_rows // node_rows
    local_rows = stored_rows % node_rows
    position_ids = jnp.arange(sampled, dtype=jnp.int32)
    earlier = position_ids[None, :] < position_ids[:, None]
    same_device = elem_device[None, :] == elem_device[:, None]
    in_group = earlier & same_device
    slot_ids = jnp.sum(in_group.astype(jnp.int32), axis=1)
    owner_ids = jnp.arange(devices, dtype=jnp.int32)
    owned_mask = jnp.any(live_nodes[:, :, None] & (owners[:, :, None] == owner_ids), axis=1).astype(
        jnp.float32
    )
    ranks_by_owner = jnp.dot(
        in_group.astype(jnp.float32), owned_mask, precision=lax.Precision.HIGHEST
    ).astype(jnp.int32)
    peer_ranks = jnp.take_along_axis(ranks_by_owner, owners, axis=1)
    sending = live_nodes & (owners == elem_rank)
    target = jnp.where(sending, elem_device[:, None], devices)
    row_table = (
        jnp.full((devices, pair_bound), -1, jnp.int32)
        .at[target, peer_ranks]
        .set(local_rows, mode="drop")
    )
    send_rows = node_basis[jnp.maximum(row_table, 0)]
    outgoing = jnp.where((row_table >= 0)[:, :, None], send_rows, jnp.zeros((), jnp.bfloat16))
    incoming = lax.all_to_all(outgoing, "elem", split_axis=0, concat_axis=0, tiled=True)
    at_device = elem_device == elem_rank
    slot_index = jnp.where(at_device, slot_ids, capacity)
    slot_elem = (
        jnp.full((capacity,), sampled, jnp.int32).at[slot_index].set(position_ids, mode="drop")
    )
    slot_live = slot_elem < sampled
    picked = jnp.minimum(slot_elem, sampled - 1)
    slot_rows = incoming[owners[picked], jnp.minimum(peer_ranks[picked], pair_bound - 1)]
    slot_mask = live_nodes[picked] & slot_live[:, None]
    local_basis = jnp.where(slot_mask[:, :, None], slot_rows, jnp.zeros((), jnp.bfloat16))
    element_basis = local_basis.reshape(capacity, ENODES * NDOF, MODES)
    displaced = jnp.einsum(
        "ekm,ms->eks", element_basis, reduced_coords, preferred_element_type=jnp.float32
    ).astype(jnp.bfloat16)
    forces = jnp.einsum(
        "tkl,els->ekst", stiff_terms, displaced, preferred_element_type=jnp.float32
    ).astype(jnp.bfloat16)
    forces = forces.reshape(capacity, ENODES * NDOF, -1)
    projected = jnp.einsum(
        "ekm,ekc->emc", element_basis, forces, preferred_element_type=jnp.float32
    ).astype(jnp.bfloat16)
    banded = lax.all_to_all(projected, "snap", split_axis=1, concat_axis=2, tiled=True)
    band_rows = banded.reshape(-1, banded.shape[2])
    columns = band_rows.shape[1]
    total_rows = sampled * MODES
    partial_gram = lax.dot_general(
        band_rows, band_rows, (((0,), (0,)), ((), ())), preferred_element_type=jnp.float32
    )
    gram_matrix = lax.psum(partial_gram, ("elem", "snap"))
    gram_matrix = gram_matrix / total_rows
    lower_factor = jnp.linalg.cholesky(gram_matrix)
    identity_matrix = jnp.eye(columns, dtype=jnp.float32)
    lower_inverse = jax.scipy.linalg.solve_triangular(lower_factor, identity_matrix, lower=True)
    ortho_rows = lax.dot_general(
        band_rows.astype(jnp.float32),
        lower_inverse,
        (((1,), (1,)), ((), ())),
        precision=lax.Precision.HIGHEST,
        preferred_element_type=jnp.float32,
    )
    share = columns // devices
    upper_rows = lax.dynamic_slice_in_dim(lower_factor.T, elem_rank * share, share, 0)
    return (ortho_rows.reshape(banded.shape), upper_rows)


def solution(mesh):
    placed = (P("elem", None), P(), P(None, "snap"), P(), P(), P(), P())
    return jax.shard_map(
        shards,
        mesh=mesh,
        in_specs=placed,
        out_specs=(P("elem", "snap", None), P("elem", None)),
        check_vma=False,
    )
```

profile of v0, /device:TPU:2, one launch (start us, length us, event | category | flops | bytes accessed | tf_op | source)
XLA Modules:
  0.0 630.0 jit_solution(7660797386319666554)
XLA Ops:
  10.3 2.9 gather_fusion
  15.9 23.0 %gather_fusion.2 = s32[4096]{0:T(1024)S(1)} fusion(s32[65536]{0:T(1024)S(1)} %copy-done.1, s32[4096]{0:T(1024)S(1)} %broadcast_clamp_fusion), kind=kCustom, calls=%fused_computation.2 | custom fusion | bytes 49152 | tf_op jit(solution)/shard_map/gather | solution.py:22
  48.0 33.0 %gather_fusion.7 = s32[4096]{0:T(1024)S(1)} fusion(s32[512,64]{0,1:T(8,128)S(1)} %convolution_convert_fusion.2, s32[4096]{0:T(1024)S(1)} %reshape.363), kind=kCustom, calls=%fused_computation.7 | custom fusion | bytes 65536 | tf_op jit(solution)/shard_map/jit(take_along_axis)/gather | solution.py:37
  88.4 15.5 %scatter_custom_fusion.1 = s32[128]{0:T(128)S(1)} fusion(s32[4096]{0:T(1024)S(1)} %reshape.377, s32[4096]{0:T(1024)S(1)} %reshape.379, s32[]{:T(128)} %constant.211.clone.1), kind=kCustom, calls=%fused_computation.155 | custom fusion | bytes 516
  109.7 12.1 %all-to-all-start = ((bf16[64,2,1536]{2,1,0:T(2,128)(2,1)}), bf16[64,2,1536]{2,1,0:T(2,128)(2,1)S(1)}, u32[]{:S(2)}, u32[]{:S(2)}) async-start(bf16[64,2,1536]{2,1,0:T(2,128)(2,1)} %broadcast_select_fusion), calls=%async_computation | async-start | bytes 786432 | tf_op jit(solution)/shard_map/all_to_all | solution.py:47
  124.7 3.2 scatter_custom_fusion
  151.1 29.8 %all_to_all.20 = bf16[16,512,128]{2,0,1:T(8,128)(2,1)} all-to-all(bf16[16,512,128]{2,0,1:T(8,128)(2,1)S(1)} %copy.125), channel_id=1, replica_groups=mesh['elem'=64,'snap'=4] {'snap'}, dimensions={1} | all-to-all | bytes 4194304 | tf_op jit(solution)/shard_map/all_to_all | solution.py:69
  180.9 5.1 copy.126
  186.0 4.5 fusion
  192.4 4.5 copy.127
  197.0 4.3 dot_general.24
  201.3 248.6 %all-reduce.3.cloned.1.call-done = f32[512,512]{0,1:T(8,128)} async-done(((f32[512,512]{0,1:T(8,128)}), f32[512,512]{0,1:T(8,128)}) %all-reduce.3.cloned.1.call-update) | async-done | bytes 1048592 | tf_op jit(solution)/shard_map/psum | solution.py:76
  457.4 11.7 %cholesky.104 = f32[128,128]{1,0:T(8,128)S(1)} custom-call(f32[128,128]{1,0:T(8,128)S(1)} %cholesky.266), custom_call_target="Cholesky" | custom-call | tf_op jit(solution)/shard_map/jit(cholesky)/cholesky | solution.py:78
  469.7 9.8 %custom-call.31 = f32[1,128,128]{1,2,0:T(8,128)S(1)} custom-call(f32[1,128,128]{2,1,0:T(8,128)S(1)} %get-tuple-element.47), custom_call_target="InvertDiagBlocksLowerTriangular" | custom-call | tf_op jit(solution)/shard_map/jit(cholesky)/cholesky | solution.py:78
  484.0 11.7 %cholesky.217 = f32[128,128]{1,0:T(8,128)S(1)} custom-call(f32[128,128]{1,0:T(8,128)S(1)} %cholesky.270), custom_call_target="Cholesky" | custom-call | tf_op jit(solution)/shard_map/jit(cholesky)/cholesky | solution.py:78
  499.0 10.2 %custom-call.32 = f32[1,128,128]{1,2,0:T(8,128)S(1)} custom-call(f32[1,128,128]{2,1,0:T(8,128)S(1)} %get-tuple-element.44), custom_call_target="InvertDiagBlocksLowerTriangular" | custom-call | tf_op jit(solution)/shard_map/jit(cholesky)/cholesky | solution.py:78
  512.5 11.7 %cholesky.238 = f32[128,128]{1,0:T(8,128)S(1)} custom-call(f32[128,128]{1,0:T(8,128)S(1)} %cholesky.275), custom_call_target="Cholesky" | custom-call | tf_op jit(solution)/shard_map/jit(cholesky)/cholesky | solution.py:78
  525.5 9.8 %custom-call.33 = f32[1,128,128]{1,2,0:T(8,128)S(1)} custom-call(f32[1,128,128]{2,1,0:T(8,128)S(1)} %get-tuple-element.41), custom_call_target="InvertDiagBlocksLowerTriangular" | custom-call | tf_op jit(solution)/shard_map/jit(cholesky)/cholesky | solution.py:78
  537.6 11.9 %cholesky.255 = f32[128,128]{1,0:T(8,128)S(1)} custom-call(f32[128,128]{1,0:T(8,128)S(1)} %convolution_subtract_fusion.5), custom_call_target="Cholesky" | custom-call | tf_op jit(solution)/shard_map/jit(cholesky)/cholesky | solution.py:78
  557.2 13.5 %while.1 = (s32[]{:T(128)}, f32[512,512]{1,0:T(8,128)}, s32[4,2]{0,1:T(2,128)S(1)}, f32[4,128,128]{2,1,0:T(8,128)}, s32[]{:T(128)}) while((s32[]{:T(128)}, f32[512,512]{1,0:T(8,128)}, s32[4,2]{0,1:T(2,128)S(1)}, f32[4,128,128]{2,1,0:T(8,128)}, s32[]{:T(128)}) %tuple.39), condition=%wide.while_cond, body=%wide.while_body.sunk | while | flops 2 | bytes 132205 | solution.py:80
  557.8 2.8 bitcast_dynamic-update-slice_fusion.2
  561.2 2.8 bitcast_dynamic-update-slice_fusion.2
  570.7 40.1 %custom-call.34 = f32[4,128,128]{1,2,0:T(8,128)S(1)} custom-call(f32[4,128,128]{2,1,0:T(8,128)} %get-tuple-element.9), custom_call_target="InvertDiagBlocksLowerTriangular" | custom-call | tf_op jit(solution)/shard_map/jit(_solve_triangular)/triangular_solve | solution.py:80
  617.9 5.1 fusion.4
  (137 shorter events, 98.7 us)
Async XLA Ops:
  7.2 97.9 %copy-start = (bf16[1024,1536]{1,0:T(8,128)(2,1)S(1)}, bf16[1024,1536]{1,0:T(8,128)(2,1)}, u32[]{:S(2)}) copy-start(bf16[1024,1536]{1,0:T(8,128)(2,1)} %param.7) | copy-start | bytes 9437188
  8.0 7.9 %copy-start.1 = (s32[65536]{0:T(1024)S(1)}, s32[65536]{0:T(1024)}, u32[]{:S(2)}) copy-start(s32[65536]{0:T(1024)} %param.12) | copy-start | bytes 786436
  39.0 8.6 %copy-start.8 = (s32[512]{0:T(512)S(1)}, s32[512]{0:T(512)}, u32[]{:S(2)}) copy-start(s32[512]{0:T(512)} %param.13) | copy-start | bytes 6148
  40.0 1.9 copy-start.5
  41.9 40.0 %copy-start.6 = (pred[512,8]{1,0:T(8,128)(4,1)}, pred[512,8]{1,0:T(8,128)(4,1)S(1)}, u32[]{:S(2)}) copy-start(pred[512,8]{1,0:T(8,128)(4,1)S(1)} %get-tuple-element.33) | copy-start | bytes 12292
  43.1 1.3 copy-start.4
  47.9 38.2 %copy-start.10 = (s32[2]{0:T(128)S(1)}, s32[2]{0:T(128)}, u32[]{:S(2)}) copy-start(s32[2]{0:T(128)} %constant.235) | copy-start | bytes 28
  48.0 38.2 %copy-start.9 = (s32[2]{0:T(128)S(1)}, s32[2]{0:T(128)}, u32[]{:S(2)}) copy-start(s32[2]{0:T(128)} %constant.232) | copy-start | bytes 28
  109.7 32.5 %all-to-all-start = ((bf16[64,2,1536]{2,1,0:T(2,128)(2,1)}), bf16[64,2,1536]{2,1,0:T(2,128)(2,1)S(1)}, u32[]{:S(2)}, u32[]{:S(2)}) async-start(bf16[64,2,1536]{2,1,0:T(2,128)(2,1)} %broadcast_select_fusion), calls=%async_computation | async-start | bytes 786432 | tf_op jit(solution)/shard_map/all_to_all | solution.py:47
  121.8 328.0 %all-reduce.3.cloned.1.call-start = ((), (), s32[]{:S(2)}) async-start(), calls=%async_computation.2 | async-start | bytes 2097152 | tf_op jit(solution)/shard_map/psum | solution.py:76
  456.4 1.0 copy-start.3
  469.1 0.6 copy-start.7
  613.3 4.6 copy-start.2
Sparse Core Ops, SparseCore 0:
  190.6 259.1 all-reduce.2
where the time goes:
time: 638 us; the launch traced here: 630 us
  waiting for transfers between devices  249 us (39%)
  other arithmetic  149 us (23%)
  local copies, waits for them, and re-layouts  143 us (22%)
  matrix products  29.9 us (5%)
  blocking collectives  29.8 us (5%)
  between operations  17.2 us (3%)
  starting transfers between devices  12.1 us (2%)
    psum x1, waiting for transfers between devices, shards(): gram_matrix = lax.psum(partial_gram, ('elem', 'snap'))  249 us
    another operation x14, other arithmetic, shards(): lower_factor = jnp.linalg.cholesky(gram_matrix)  80.7 us
    another operation x3, other arithmetic, shards(): jax.scipy.linalg.solve_triangular(lower_factor, identity_matrix, lower=True)  42.6 us
    gather x4, local copies, waits for them, and re-layouts, shards(): peer_ranks = jnp.take_along_axis(ranks_by_owner, owners, axis=1)  35.9 us
    all_to_all x1, blocking collectives, shards(): lax.all_to_all(projected, 'snap', split_axis=1, concat_axis=2, tiled=True)  29.8 us
    gather x3, local copies, waits for them, and re-layouts, shards(): stored_rows = jnp.where(live_nodes, node_slot[jnp.maximum(node_ids, 0)], 0)  24.1 us
    unnamed x28, local copies, waits for them, and re-layouts  21.4 us
    another operation x12, local copies, waits for them, and re-layouts  13.5 us
  transfers between devices with their start and end apart: 2, of which 1 were waited for; matrix products, arithmetic and copies ran while one was open for 5% of the time, Pallas kernels for 0%

commit v1 on v0

--- a/solution.py
+++ b/solution.py
@@ -73,7 +73,9 @@
     partial_gram = lax.dot_general(
         band_rows, band_rows, (((0,), (0,)), ((), ())), preferred_element_type=jnp.float32
     )
-    gram_matrix = lax.psum(partial_gram, ("elem", "snap"))
+    gram_matrix = partial_gram
+    for name in ("snap", "elem"):
+        gram_matrix = lax.psum(gram_matrix, name)
     gram_matrix = gram_matrix / total_rows
     lower_factor = jnp.linalg.cholesky(gram_matrix)
     identity_matrix = jnp.eye(columns, dtype=jnp.float32)

time: 638 us -> 623 us (0.976)
  waiting for transfers between devices: 249 us -> 233 us
    psum x1 -> x2, waiting for transfers between devices: 249 us -> 233 us  [shards(): gram_matrix = lax.psum(gram_matrix, name)]
  transfers between devices with their start and end apart: 2 -> 3, of which waited for: 1 -> 2; matrix products, arithmetic and copies ran while one was open for 5% -> 5% of each run, Pallas kernels for 0% -> 0%
where the time goes in v1:
time: 623 us; the launch traced here: 614 us
  waiting for transfers between devices  233 us (37%)
  other arithmetic  149 us (24%)
  local copies, waits for them, and re-layouts  143 us (23%)
  matrix products  29.9 us (5%)
  blocking collectives  29.8 us (5%)
  between operations  17.2 us (3%)
  starting transfers between devices  12.2 us (2%)
    psum x2, waiting for transfers between devices, shards(): gram_matrix = lax.psum(gram_matrix, name)  233 us
    another operation x14, other arithmetic, shards(): lower_factor = jnp.linalg.cholesky(gram_matrix)  80.7 us
    another operation x3, other arithmetic, shards(): jax.scipy.linalg.solve_triangular(lower_factor, identity_matrix, lower=True)  42.6 us
    gather x4, local copies, waits for them, and re-layouts, shards(): peer_ranks = jnp.take_along_axis(ranks_by_owner, owners, axis=1)  35.9 us
    all_to_all x1, blocking collectives, shards(): lax.all_to_all(projected, 'snap', split_axis=1, concat_axis=2, tiled=True)  29.8 us
    gather x3, local copies, waits for them, and re-layouts, shards(): stored_rows = jnp.where(live_nodes, node_slot[jnp.maximum(node_ids, 0)], 0)  24.1 us
    unnamed x28, local copies, waits for them, and re-layouts  21.4 us
    another operation x12, local copies, waits for them, and re-layouts  13.5 us
  transfers between devices with their start and end apart: 3, of which 2 were waited for; matrix products, arithmetic and copies ran while one was open for 5% of the time, Pallas kernels for 0%

profile of v1, /device:TPU:2, one launch (start us, length us, event | category | flops | bytes accessed | tf_op | source)
XLA Modules:
  0.0 614.4 jit_solution(17505741598922533651)
XLA Ops:
  10.3 2.9 gather_fusion
  15.9 23.0 %gather_fusion.2 = s32[4096]{0:T(1024)S(1)} fusion(s32[65536]{0:T(1024)S(1)} %copy-done.1, s32[4096]{0:T(1024)S(1)} %broadcast_clamp_fusion), kind=kCustom, calls=%fused_computation.2 | custom fusion | bytes 49152 | tf_op jit(solution)/shard_map/gather | solution.py:22
  48.0 33.0 %gather_fusion.7 = s32[4096]{0:T(1024)S(1)} fusion(s32[512,64]{0,1:T(8,128)S(1)} %convolution_convert_fusion.2, s32[4096]{0:T(1024)S(1)} %reshape.363), kind=kCustom, calls=%fused_computation.7 | custom fusion | bytes 65536 | tf_op jit(solution)/shard_map/jit(take_along_axis)/gather | solution.py:37
  88.4 15.5 %scatter_custom_fusion.1 = s32[128]{0:T(128)S(1)} fusion(s32[4096]{0:T(1024)S(1)} %reshape.377, s32[4096]{0:T(1024)S(1)} %reshape.379, s32[]{:T(128)} %constant.211.clone.1), kind=kCustom, calls=%fused_computation.155 | custom fusion | bytes 516
  109.7 12.1 %all-to-all-start = ((bf16[64,2,1536]{2,1,0:T(2,128)(2,1)}), bf16[64,2,1536]{2,1,0:T(2,128)(2,1)S(1)}, u32[]{:S(2)}, u32[]{:S(2)}) async-start(bf16[64,2,1536]{2,1,0:T(2,128)(2,1)} %broadcast_select_fusion), calls=%async_computation | async-start | bytes 786432 | tf_op jit(solution)/shard_map/all_to_all | solution.py:47
  124.7 3.2 scatter_custom_fusion
  151.1 29.8 %all_to_all.20 = bf16[16,512,128]{2,0,1:T(8,128)(2,1)} all-to-all(bf16[16,512,128]{2,0,1:T(8,128)(2,1)S(1)} %copy.125), channel_id=1, replica_groups=mesh['elem'=64,'snap'=4] {'snap'}, dimensions={1} | all-to-all | bytes 4194304 | tf_op jit(solution)/shard_map/all_to_all | solution.py:69
  180.9 5.1 copy.126
  186.0 4.5 fusion
  190.6 51.0 %all-reduce.4.cloned.1.call-done = f32[512,512]{0,1:T(8,128)} async-done(((f32[512,512]{0,1:T(8,128)}), f32[512,512]{0,1:T(8,128)}) %all-reduce.4.cloned.1.call-update) | async-done | bytes 1048592 | tf_op jit(solution)/shard_map/psum | solution.py:78
  243.5 4.5 copy.127
  248.0 4.3 dot_general.24
  252.3 181.9 %all-reduce.6.cloned.1.call-done = f32[512,512]{0,1:T(8,128)} async-done(((f32[512,512]{0,1:T(8,128)}), f32[512,512]{0,1:T(8,128)}) %all-reduce.6.cloned.1.call-update) | async-done | bytes 1048592 | tf_op jit(solution)/shard_map/psum | solution.py:78
  441.8 11.7 %cholesky.104 = f32[128,128]{1,0:T(8,128)S(1)} custom-call(f32[128,128]{1,0:T(8,128)S(1)} %cholesky.266), custom_call_target="Cholesky" | custom-call | tf_op jit(solution)/shard_map/jit(cholesky)/cholesky | solution.py:80
  454.1 9.8 %custom-call.31 = f32[1,128,128]{1,2,0:T(8,128)S(1)} custom-call(f32[1,128,128]{2,1,0:T(8,128)S(1)} %get-tuple-element.47), custom_call_target="InvertDiagBlocksLowerTriangular" | custom-call | tf_op jit(solution)/shard_map/jit(cholesky)/cholesky | solution.py:80
  468.4 11.7 %cholesky.217 = f32[128,128]{1,0:T(8,128)S(1)} custom-call(f32[128,128]{1,0:T(8,128)S(1)} %cholesky.270), custom_call_target="Cholesky" | custom-call | tf_op jit(solution)/shard_map/jit(cholesky)/cholesky | solution.py:80
  483.4 10.2 %custom-call.32 = f32[1,128,128]{1,2,0:T(8,128)S(1)} custom-call(f32[1,128,128]{2,1,0:T(8,128)S(1)} %get-tuple-element.44), custom_call_target="InvertDiagBlocksLowerTriangular" | custom-call | tf_op jit(solution)/shard_map/jit(cholesky)/cholesky | solution.py:80
  496.9 11.7 %cholesky.238 = f32[128,128]{1,0:T(8,128)S(1)} custom-call(f32[128,128]{1,0:T(8,128)S(1)} %cholesky.275), custom_call_target="Cholesky" | custom-call | tf_op jit(solution)/shard_map/jit(cholesky)/cholesky | solution.py:80
  509.9 9.8 %custom-call.33 = f32[1,128,128]{1,2,0:T(8,128)S(1)} custom-call(f32[1,128,128]{2,1,0:T(8,128)S(1)} %get-tuple-element.41), custom_call_target="InvertDiagBlocksLowerTriangular" | custom-call | tf_op jit(solution)/shard_map/jit(cholesky)/cholesky | solution.py:80
  522.0 11.9 %cholesky.255 = f32[128,128]{1,0:T(8,128)S(1)} custom-call(f32[128,128]{1,0:T(8,128)S(1)} %convolution_subtract_fusion.5), custom_call_target="Cholesky" | custom-call | tf_op jit(solution)/shard_map/jit(cholesky)/cholesky | solution.py:80
  541.6 13.5 %while.1 = (s32[]{:T(128)}, f32[512,512]{1,0:T(8,128)}, s32[4,2]{0,1:T(2,128)S(1)}, f32[4,128,128]{2,1,0:T(8,128)}, s32[]{:T(128)}) while((s32[]{:T(128)}, f32[512,512]{1,0:T(8,128)}, s32[4,2]{0,1:T(2,128)S(1)}, f32[4,128,128]{2,1,0:T(8,128)}, s32[]{:T(128)}) %tuple.39), condition=%wide.while_cond, body=%wide.while_body.sunk | while | flops 2 | bytes 132205 | solution.py:82
  542.2 2.8 bitcast_dynamic-update-slice_fusion.2
  555.1 40.1 %custom-call.34 = f32[4,128,128]{1,2,0:T(8,128)S(1)} custom-call(f32[4,128,128]{2,1,0:T(8,128)} %get-tuple-element.9), custom_call_target="InvertDiagBlocksLowerTriangular" | custom-call | tf_op jit(solution)/shard_map/jit(_solve_triangular)/triangular_solve | solution.py:82
  602.3 5.1 fusion.4
  (140 shorter events, 101.5 us)
Async XLA Ops:
  7.2 97.9 %copy-start = (bf16[1024,1536]{1,0:T(8,128)(2,1)S(1)}, bf16[1024,1536]{1,0:T(8,128)(2,1)}, u32[]{:S(2)}) copy-start(bf16[1024,1536]{1,0:T(8,128)(2,1)} %param.7) | copy-start | bytes 9437188
  8.0 7.9 %copy-start.1 = (s32[65536]{0:T(1024)S(1)}, s32[65536]{0:T(1024)}, u32[]{:S(2)}) copy-start(s32[65536]{0:T(1024)} %param.12) | copy-start | bytes 786436
  39.0 8.6 %copy-start.8 = (s32[512]{0:T(512)S(1)}, s32[512]{0:T(512)}, u32[]{:S(2)}) copy-start(s32[512]{0:T(512)} %param.13) | copy-start | bytes 6148
  40.0 1.9 copy-start.5
  41.9 40.0 %copy-start.6 = (pred[512,8]{1,0:T(8,128)(4,1)}, pred[512,8]{1,0:T(8,128)(4,1)S(1)}, u32[]{:S(2)}) copy-start(pred[512,8]{1,0:T(8,128)(4,1)S(1)} %get-tuple-element.33) | copy-start | bytes 12292
  43.1 1.3 copy-start.4
  47.9 38.2 %copy-start.10 = (s32[2]{0:T(128)S(1)}, s32[2]{0:T(128)}, u32[]{:S(2)}) copy-start(s32[2]{0:T(128)} %constant.235) | copy-start | bytes 28
  48.0 38.2 %copy-start.9 = (s32[2]{0:T(128)S(1)}, s32[2]{0:T(128)}, u32[]{:S(2)}) copy-start(s32[2]{0:T(128)} %constant.232) | copy-start | bytes 28
  109.7 32.5 %all-to-all-start = ((bf16[64,2,1536]{2,1,0:T(2,128)(2,1)}), bf16[64,2,1536]{2,1,0:T(2,128)(2,1)S(1)}, u32[]{:S(2)}, u32[]{:S(2)}) async-start(bf16[64,2,1536]{2,1,0:T(2,128)(2,1)} %broadcast_select_fusion), calls=%async_computation | async-start | bytes 786432 | tf_op jit(solution)/shard_map/all_to_all | solution.py:47
  121.8 119.7 %all-reduce.4.cloned.1.call-start = ((), (), s32[]{:S(2)}) async-start(), calls=%async_computation.2 | async-start | bytes 2097152 | tf_op jit(solution)/shard_map/psum | solution.py:78
  190.5 243.7 %all-reduce.6.cloned.1.call-start = ((), (), s32[]{:S(2)}) async-start(), calls=%async_computation.3 | async-start | bytes 2097152 | tf_op jit(solution)/shard_map/psum | solution.py:78
  440.8 1.0 copy-start.3
  453.5 0.6 copy-start.7
  597.7 4.6 copy-start.2
Sparse Core Ops, SparseCore 0:
  190.6 50.8 all-reduce.3
  245.0 189.1 all-reduce.5
